TPU v7x, 32 devices: a whole 2x2x4 slice. The times are simulated.
32 devices in a mesh: dp: 8 (over z, y), tensor: 4 (over x, core).
Axes of the slice: x: 2, y: 2, z: 4, core: 2. Of those that a mesh axis runs over, the one named last changes fastest.
Arguments:
- tokens: bfloat16 [16384, 768], P(('dp', 'tensor')), may hold values from -6 to 6
- cotangent: bfloat16 [16384, 768], P(('dp', 'tensor')), may hold values from -6 to 6
- qkv_weight: float32 [3, 768, 768], P(None, 'dp', 'tensor'), may hold values from -0.21875 to 0.21875
- qv_bias: float32 [2, 768], P(None, 'tensor'), may hold values from -1.8 to 1.8
- out_weight: float32 [768, 768], P('tensor', 'dp'), may hold values from -1 to 1
- out_bias: float32 [768], replicated, may hold values from -1.8 to 1.8
- first_gain: float32 [768], replicated, may hold values from 0.5 to 1.5
- first_shift: float32 [768], replicated, may hold values from -1.2 to 1.2
- up_weight: float32 [768, 3072], P('dp', 'tensor'), may hold values from -0.21875 to 0.21875
- up_bias: float32 [3072], P('tensor'), may hold values from -1.8 to 1.8
- down_weight: float32 [3072, 768], P('tensor', 'dp'), may hold values from -0.109375 to 0.109375
- down_bias: float32 [768], replicated, may hold values from -1.8 to 1.8
- second_gain: float32 [768], replicated, may hold values from 0.5 to 1.5
- second_shift: float32 [768], replicated, may hold values from -1.2 to 1.2
- act_ranges: float32 [4], replicated, may hold values from 0.5 to 3.5, as said below
- long_lengths: int32 [8], P('dp'), may hold values from 128 to 512, as said below
- short_lengths: int32 [96], P('dp'), may hold values from 32 to 128, as said below
Outputs:
- layer_out: bfloat16 [16384, 768], P(('dp', 'tensor'))
- tokens_grad: bfloat16 [16384, 768], P(('dp', 'tensor'))
- qkv_grad: float32 [3, 768, 768], P(None, 'dp', 'tensor')
- qv_bias_grad: float32 [2, 768], P(None, 'tensor')
- out_grad: float32 [768, 768], P('tensor', 'dp')
- out_bias_grad: float32 [768], replicated
- first_gain_grad: float32 [768], replicated
- first_shift_grad: float32 [768], replicated
- up_grad: float32 [768, 3072], P('dp', 'tensor')
- up_bias_grad: float32 [3072], P('tensor')
- down_grad: float32 [3072, 768], P('tensor', 'dp')
- down_bias_grad: float32 [768], replicated
- second_gain_grad: float32 [768], replicated
- second_shift_grad: float32 [768], replicated
- new_ranges: float32 [4], replicated
Inputs may be any that keep to these rules, and one draw needn't show every extreme that they name: Each long sequence uses its first long_lengths slots; at least a quarter of 512, and some sequence uses all 512. Each short sequence uses its first short_lengths slots; at least a quarter of 128, and some sequence uses all 128. `act_ranges`: entry 1 lies in 0.5 to 0.8, the others in 2.5 to 3.5.
All inputs are finite; a program needn't handle non-finite values.
Results may differ from a plain program's by a relative error of at most 0.018.
The roundings to bfloat16 on the way count: a program that leaves them out, or rounds other values in their place, can miss the bound.
Values may be sent and summed in bfloat16 or wider, within the bound.
No kernel may reach another device: no remote copies, remote signals or barrier semaphores. Data moves between devices by JAX's collectives and lax.ppermute only.
A program may use at most 128 MiB of HBM per device.

v0:
```python
import jax
import jax.numpy as jnp
from jax import lax
from jax.sharding import PartitionSpec as P

HEAD_DIM = 64
LONG_LEN = 512
SHORT_LEN = 128
ema_decay = 0.9
epsilon = 1e-06
root_half = 0.7071067811865476
density_scale = 0.3989422804014327


def matmul_plain(left, right):
    return jnp.dot(left, right, preferred_element_type=jnp.float32)


def matmul_left_t(left, right):
    return lax.dot_general(
        left, right, (((0,), (0,)), ((), ())), preferred_element_type=jnp.float32
    )


def matmul_right_t(left, right):
    return lax.dot_general(
        left, right, (((1,), (1,)), ((), ())), preferred_element_type=jnp.float32
    )


def saturate(values, limit):
    return limit * jnp.tanh(values / limit)


def saturate_slope(values, limit):
    bent = jnp.tanh(values / limit)
    return 1.0 - bent * bent


def block_masks(long_part, short_part):
    per_block = LONG_LEN // SHORT_LEN
    position = jnp.arange(LONG_LEN, dtype=jnp.int32)
    long_segment = jnp.zeros((long_part.shape[0], LONG_LEN), jnp.int32)
    long_valid = position[None, :] < long_part[:, None]
    short_rows = short_part.reshape(-1, per_block)
    short_segment = jnp.broadcast_to(position // SHORT_LEN, (short_rows.shape[0], LONG_LEN))
    short_limit = jnp.repeat(short_rows, SHORT_LEN, axis=1)
    short_valid = (position % SHORT_LEN)[None, :] < short_limit
    return (
        jnp.concatenate([long_segment, short_segment], 0),
        jnp.concatenate([long_valid, short_valid], 0),
    )


def layer_norm_fwd(summed, gain, shift):
    average = jnp.mean(summed, axis=-1, keepdims=True)
    centered = summed - average
    inv_scale = lax.rsqrt(jnp.mean(centered * centered, axis=-1, keepdims=True) + epsilon)
    normed = centered * inv_scale
    return (normed * gain + shift, normed, inv_scale)


def norm_backward(incoming, normed, inv_scale, gain):
    scaled = incoming * gain
    row_mean = jnp.mean(scaled, axis=-1, keepdims=True)
    row_cross = jnp.mean(scaled * normed, axis=-1, keepdims=True)
    grad_in = inv_scale * (scaled - row_mean - normed * row_cross)
    return (grad_in, jnp.sum(incoming * normed, axis=0), jnp.sum(incoming, axis=0))


def gelu_slope(values):
    return (
        0.5 * (1.0 + lax.erf(values * root_half))
        + values * jnp.exp(-0.5 * values * values) * density_scale
    )


def score_block(queries, key_rows, segment, key_valid):
    scores = jnp.einsum(
        "qhd,khd->hqk", queries, key_rows, preferred_element_type=jnp.float32
    ) * HEAD_DIM ** (-0.5)
    allowed = (segment[:, None] == segment[None, :]) & key_valid[None, :]
    return jnp.where(allowed[None, :, :], scores, -1000000000.0)


def block_forward(pieces):
    queries, key_rows, values, segment, key_valid = pieces
    scores = score_block(queries, key_rows, segment, key_valid)
    row_max = jnp.max(scores, axis=-1, keepdims=True)
    expanded = jnp.exp(scores - row_max)
    row_total = jnp.sum(expanded, axis=-1, keepdims=True)
    shares = (expanded / row_total).astype(jnp.bfloat16)
    context = jnp.einsum("hqk,khd->qhd", shares, values, preferred_element_type=jnp.float32)
    return (context, (row_max + jnp.log(row_total))[:, :, 0])


def block_backward(pieces):
    queries, key_rows, values, segment, key_valid, log_total, grad_ctx = pieces
    score_scale = HEAD_DIM ** (-0.5)
    scores = score_block(queries, key_rows, segment, key_valid)
    shares = jnp.exp(scores - log_total[:, :, None])
    grad_shares = jnp.einsum("qhd,khd->hqk", grad_ctx, values, preferred_element_type=jnp.float32)
    row_inner = jnp.sum(shares * grad_shares, axis=-1, keepdims=True)
    grad_scores = (shares * (grad_shares - row_inner)).astype(jnp.bfloat16)
    grad_values = jnp.einsum(
        "hqk,qhd->khd", shares.astype(jnp.bfloat16), grad_ctx, preferred_element_type=jnp.float32
    )
    grad_queries = (
        jnp.einsum("hqk,khd->qhd", grad_scores, key_rows, preferred_element_type=jnp.float32)
        * score_scale
    )
    grad_keys = (
        jnp.einsum("hqk,qhd->khd", grad_scores, queries, preferred_element_type=jnp.float32)
        * score_scale
    )
    return (
        grad_queries.astype(jnp.bfloat16),
        grad_keys.astype(jnp.bfloat16),
        grad_values.astype(jnp.bfloat16),
    )


def body(
    tokens,
    cotangent,
    qkv_weight,
    qv_bias,
    out_weight,
    out_bias,
    first_gain,
    first_shift,
    up_weight,
    up_bias,
    down_weight,
    down_bias,
    second_gain,
    second_shift,
    act_ranges,
    long_lengths,
    short_lengths,
):
    tensor_lanes = lax.axis_size("tensor")
    column = lax.axis_index("tensor")
    shard_rows = tokens.shape[0]
    group_rows = shard_rows * tensor_lanes
    head_cols = qkv_weight.shape[2]
    up_cols = up_weight.shape[1]
    blocked = (group_rows // LONG_LEN, LONG_LEN, head_cols // HEAD_DIM, HEAD_DIM)
    masters = (
        qkv_weight.astype(jnp.bfloat16),
        out_weight.astype(jnp.bfloat16),
        up_weight.astype(jnp.bfloat16),
        down_weight.astype(jnp.bfloat16),
    )
    qkv_full, out_full, up_full, down_full = (
        lax.all_gather(masters[0], "dp", axis=1, tiled=True),
        lax.all_gather(masters[1], "dp", axis=1, tiled=True),
        lax.all_gather(masters[2], "dp", axis=0, tiled=True),
        lax.all_gather(masters[3], "dp", axis=1, tiled=True),
    )
    inputs = tokens.astype(jnp.float32)
    in_clip = jnp.clip(inputs, -act_ranges[0], act_ranges[0]).astype(jnp.bfloat16)
    in_rows = lax.all_gather(in_clip, "tensor", axis=0, tiled=True)
    projected = jnp.einsum("td,jde->jte", in_rows, qkv_full, preferred_element_type=jnp.float32)
    queries = (projected[0] + qv_bias[0]).astype(jnp.bfloat16).reshape(blocked)
    key_rows = projected[1].astype(jnp.bfloat16).reshape(blocked)
    values = (projected[2] + qv_bias[1]).astype(jnp.bfloat16).reshape(blocked)
    segment, key_valid = block_masks(long_lengths, short_lengths)
    context, log_total = lax.map(block_forward, (queries, key_rows, values, segment, key_valid))
    context = context.reshape(group_rows, head_cols)
    ctx_clip = saturate(context, act_ranges[1]).astype(jnp.bfloat16)
    attn_sum = lax.psum_scatter(
        matmul_plain(ctx_clip, out_full).astype(jnp.bfloat16),
        "tensor",
        scatter_dimension=0,
        tiled=True,
    ).astype(jnp.float32)
    first_sum = inputs + attn_sum + out_bias
    middle, first_normed, first_inv = layer_norm_fwd(first_sum, first_gain, first_shift)
    mid_clip = saturate(middle, act_ranges[2]).astype(jnp.bfloat16)
    mid_rows = lax.all_gather(mid_clip, "tensor", axis=0, tiled=True)
    up_out = matmul_plain(mid_rows, up_full) + up_bias
    hidden = jax.nn.gelu(up_out, approximate=False)
    act_clip = saturate(hidden, act_ranges[3]).astype(jnp.bfloat16)
    ffn_sum = lax.psum_scatter(
        matmul_plain(act_clip, down_full).astype(jnp.bfloat16),
        "tensor",
        scatter_dimension=0,
        tiled=True,
    ).astype(jnp.float32)
    second_sum = middle + ffn_sum + down_bias
    layer_out, second_normed, second_inv = layer_norm_fwd(second_sum, second_gain, second_shift)
    maxima = lax.pmax(
        (
            jnp.max(jnp.abs(inputs)),
            jnp.max(jnp.abs(context)),
            jnp.max(jnp.abs(middle)),
            jnp.max(jnp.abs(hidden)),
        ),
        ("dp", "tensor"),
    )
    new_ranges = ema_decay * act_ranges + (1.0 - ema_decay) * jnp.stack(maxima)
    grad_second, second_gain_part, second_shift_part = norm_backward(
        cotangent.astype(jnp.float32), second_normed, second_inv, second_gain
    )
    down_rows = lax.all_gather(grad_second.astype(jnp.bfloat16), "tensor", axis=0, tiled=True)
    qkv_back, out_back, up_back, down_back = (
        lax.all_gather(masters[0], "dp", axis=1, tiled=True),
        lax.all_gather(masters[1], "dp", axis=1, tiled=True),
        lax.all_gather(masters[2], "dp", axis=0, tiled=True),
        lax.all_gather(masters[3], "dp", axis=1, tiled=True),
    )
    down_grad = matmul_left_t(act_clip, down_rows)
    grad_act = matmul_right_t(down_rows, down_back) * saturate_slope(hidden, act_ranges[3])
    grad_up = (grad_act * gelu_slope(up_out)).astype(jnp.bfloat16)
    up_grad = matmul_left_t(mid_rows, grad_up)
    mid_sum = lax.psum_scatter(
        matmul_right_t(grad_up, up_back).astype(jnp.bfloat16),
        "tensor",
        scatter_dimension=0,
        tiled=True,
    ).astype(jnp.float32)
    grad_middle = grad_second + mid_sum * saturate_slope(middle, act_ranges[2])
    grad_first, first_gain_part, first_shift_part = norm_backward(
        grad_middle, first_normed, first_inv, first_gain
    )
    attn_rows = lax.all_gather(grad_first.astype(jnp.bfloat16), "tensor", axis=0, tiled=True)
    out_grad = matmul_left_t(ctx_clip, attn_rows)
    grad_ctx = (
        matmul_right_t(attn_rows, out_back) * saturate_slope(context, act_ranges[1])
    ).astype(jnp.bfloat16)
    grad_queries, grad_keys, grad_values = lax.map(
        block_backward,
        (queries, key_rows, values, segment, key_valid, log_total, grad_ctx.reshape(blocked)),
    )
    stacked = jnp.stack(
        [
            grad_queries.reshape(group_rows, head_cols),
            grad_keys.reshape(group_rows, head_cols),
            grad_values.reshape(group_rows, head_cols),
        ]
    )
    qkv_grad = jnp.einsum("td,jte->jde", in_rows, stacked, preferred_element_type=jnp.float32)
    input_sum = lax.psum_scatter(
        jnp.einsum("jte,jde->td", stacked, qkv_back, preferred_element_type=jnp.float32).astype(
            jnp.bfloat16
        ),
        "tensor",
        scatter_dimension=0,
        tiled=True,
    ).astype(jnp.float32)
    tokens_grad = (grad_first + jnp.where(jnp.abs(inputs) <= act_ranges[0], input_sum, 0.0)).astype(
        jnp.bfloat16
    )
    qkv_grad, out_grad, up_grad, down_grad = (
        lax.psum_scatter(qkv_grad, "dp", scatter_dimension=1, tiled=True),
        lax.psum_scatter(out_grad, "dp", scatter_dimension=1, tiled=True),
        lax.psum_scatter(up_grad, "dp", scatter_dimension=0, tiled=True),
        lax.psum_scatter(down_grad, "dp", scatter_dimension=1, tiled=True),
    )
    lane_hot = (jnp.arange(tensor_lanes) == column).astype(jnp.float32)

    def spread(vector_piece):
        return (lane_hot[:, None] * vector_piece[None, :]).reshape(-1)

    query_bias_part = jnp.sum(stacked[0].astype(jnp.float32), axis=0)
    value_bias_part = jnp.sum(stacked[2].astype(jnp.float32), axis=0)
    up_bias_part = jnp.sum(grad_up.astype(jnp.float32), axis=0)
    shared = jnp.stack(
        [
            jnp.sum(grad_first, axis=0),
            first_gain_part,
            first_shift_part,
            jnp.sum(grad_second, axis=0),
            second_gain_part,
            second_shift_part,
        ]
    )
    query_total, value_total, up_total, shared_total = lax.psum(
        (spread(query_bias_part), spread(value_bias_part), spread(up_bias_part), shared),
        ("dp", "tensor"),
    )
    qv_bias_grad = jnp.stack(
        [
            lax.dynamic_slice_in_dim(query_total, column * head_cols, head_cols),
            lax.dynamic_slice_in_dim(value_total, column * head_cols, head_cols),
        ]
    )
    up_bias_grad = lax.dynamic_slice_in_dim(up_total, column * up_cols, up_cols)
    return (
        layer_out.astype(jnp.bfloat16),
        tokens_grad,
        qkv_grad,
        qv_bias_grad,
        out_grad,
        shared_total[0],
        shared_total[1],
        shared_total[2],
        up_grad,
        up_bias_grad,
        down_grad,
        shared_total[3],
        shared_total[4],
        shared_total[5],
        new_ranges,
    )


def solution(mesh):
    in_specs = (
        P(("dp", "tensor"), None),
        P(("dp", "tensor"), None),
        P(None, "dp", "tensor"),
        P(None, "tensor"),
        P("tensor", "dp"),
        P(),
        P(),
        P(),
        P("dp", "tensor"),
        P("tensor"),
        P("tensor", "dp"),
        P(),
        P(),
        P(),
        P(),
        P("dp"),
        P("dp"),
    )
    out_specs = (
        P(("dp", "tensor"), None),
        P(("dp", "tensor"), None),
        P(None, "dp", "tensor"),
        P(None, "tensor"),
        P("tensor", "dp"),
        P(),
        P(),
        P(),
        P("dp", "tensor"),
        P("tensor"),
        P("tensor", "dp"),
        P(),
        P(),
        P(),
        P(),
    )
    return jax.shard_map(body, mesh=mesh, in_specs=in_specs, out_specs=out_specs, check_vma=False)
```

profile of v0, /device:TPU:0, one launch (start us, length us, event | category | flops | bytes accessed | tf_op | source)
XLA Modules:
  0.0 788.6 jit_solution(17839399608265176750)
XLA Ops:
  10.0 2.8 fusion.80
  14.0 38.9 %all_gather.29 = bf16[3,768,192]{2,0,1:T(4,128)(2,1)S(1)} all-gather(bf16[3,96,192]{2,0,1:T(4,128)(2,1)S(1)} %copy.88), channel_id=1, replica_groups=mesh['dp'=8,'tensor'=4] {'dp'}, dimensions={1}, use_global_device_ids=true | all-gather | bytes 995328 | tf_op jit(solution)/shard_map/all_gather | solution.py:156
  52.9 2.0 copy.89
  56.7 31.1 %all_gather.30 = bf16[192,768]{0,1:T(8,128)(2,1)S(1)} all-gather(bf16[192,96]{0,1:T(8,128)(2,1)S(1)} %copy.94), channel_id=1, replica_groups=mesh['dp'=8,'tensor'=4] {'dp'}, dimensions={1}, use_global_device_ids=true | all-gather | bytes 331776 | tf_op jit(solution)/shard_map/all_gather | solution.py:157
  87.7 4.1 fusion.104
  93.3 3.2 squeeze.75
  96.5 2.2 squeeze.76
  99.4 2.9 fusion.83
  102.4 16.9 %while.26 = (s32[]{:T(128)}, f32[4,512,3,64]{1,3,2,0:T(8,128)}, f32[4,3,512]{2,1,0:T(4,128)}, bf16[4,512,3,64]{1,3,2,0:T(8,128)(2,1)S(1)}, s32[4,512]{1,0:T(4,12...) while((s32[]{:T(128)}, f32[4,512,3,64]{1,3,2,0:T(8,128)}, ...), condition=%wide.region_3.4_spmd, body=%wide.region_0.3_spmd.sunk | while | flops 211286528 | bytes 11534437 | solution.py:169
  104.8 1.8 fusion.151
  109.0 1.8 fusion.151
  113.2 1.8 fusion.151
  117.4 1.8 fusion.151
  119.3 4.2 abs_reduce_fusion.2
  125.2 2.7 convolution_convert_fusion.2
  128.9 36.0 %reduce-scatter.13.cloned.1.call-done = bf16[512,768]{1,0:T(8,128)(2,1)} async-done(((bf16[2048,768]{1,0:T(8,128)(2,1)}), bf16[512,768]{1,0:T(8,128)(2,1)}) %reduce-scatter.13.cloned.1.call-update) | async-done | bytes 786448 | tf_op jit(solution)/shard_map/reduce_scatter | solution.py:172
  165.0 1.5 fusion.88
  166.5 1.6 multiply_reduce_fusion.4
  168.7 2.9 multiply_convert_fusion.2
  171.7 1.6 convert_element_type.147
  173.4 27.0 %all-gather.9.cloned.1.call-done = bf16[2048,768]{1,0:T(8,128)(2,1)} async-done(((bf16[512,768]{1,0:T(8,128)(2,1)}), bf16[2048,768]{1,0:T(8,128)(2,1)}) %all-gather.9.cloned.1.call-update) | async-done | bytes 3145744 | tf_op jit(solution)/shard_map/all_gather | solution.py:181
  200.4 17.9 %abs_reduce_fusion = (f32[]{:T(128)}, f32[2048,768]{1,0:T(8,128)S(1)}, f32[2048,768]{1,0:T(8,128)}) fusion(f32[768]{0:T(1024)} %param.30, bf16[2048,768]{1,0:T(8,128)(2,1)} %all-gather.9.cloned.1.call-done, bf16[768,768]{1,0:T(8,128)(2,1)} %all-gather.11.cloned.1.call-done), kind=kOutput, calls=%fused_computation.74 | convolution fusion | flops 2521300992 | bytes 16911364 | tf_op jit(solution)/shard_map/dot_general | solution.py:16
  218.3 2.7 copy-done.5
  221.0 3.6 multiply_convert_fusion.1
  224.6 19.9 %all-gather.13.cloned.1.call-done = bf16[768,768]{0,1:T(8,128)(2,1)} async-done(((bf16[768,96]{0,1:T(8,128)(2,1)}), bf16[768,768]{0,1:T(8,128)(2,1)}) %all-gather.13.cloned.1.call-update) | async-done | bytes 1179664 | tf_op jit(solution)/shard_map/all_gather | solution.py:159
  244.5 6.5 convolution_convert_fusion.1
  251.5 35.7 %reduce-scatter.15.cloned.1.call-done = bf16[512,768]{1,0:T(8,128)(2,1)} async-done(((bf16[2048,768]{1,0:T(8,128)(2,1)}), bf16[512,768]{1,0:T(8,128)(2,1)}) %reduce-scatter.15.cloned.1.call-update) | async-done | bytes 786448 | tf_op jit(solution)/shard_map/reduce_scatter | solution.py:185
  287.2 2.0 fusion.101
  290.9 2.1 fusion.98
  295.3 28.6 %all-gather.15.cloned.1.call-done = bf16[2048,768]{1,0:T(8,128)(2,1)} async-done(((bf16[512,768]{1,0:T(8,128)(2,1)}), bf16[2048,768]{1,0:T(8,128)(2,1)}) %all-gather.15.cloned.1.call-update) | async-done | bytes 3145744 | tf_op jit(solution)/shard_map/all_gather | solution.py:206
  323.9 11.1 %convert_reduce_fusion = (f32[768]{0:T(1024)}, bf16[2048,768]{1,0:T(8,128)(2,1)S(1)}) fusion(f32[2048,768]{1,0:T(8,128)} %get-tuple-element.347, f32[768]{0:T(1024)} %param.30, f32[2048,768]{1,0:T(8,128)} %copy-done.5, f32[]{:T(128)} %bitcast.27, bf16[2048,768]{1,0:T(8,128)(2,1)} %all-gather.15.cloned.1.call-done, ...), kind=kOutput, calls=%fused_computation.75 | convolution fusion | flops 2442657024 | bytes 20060164 | tf_op jit(solution)/shard_map/dot_general | solution.py:26
  335.0 1.7 copy-done.31
  336.7 4.0 convolution_convert_fusion
  340.8 37.8 %reduce-scatter.17.cloned.1.call-done = bf16[512,768]{1,0:T(8,128)(2,1)} async-done(((bf16[2048,768]{1,0:T(8,128)(2,1)}), bf16[512,768]{1,0:T(8,128)(2,1)}) %reduce-scatter.17.cloned.1.call-update) | async-done | bytes 786448 | tf_op jit(solution)/shard_map/reduce_scatter | solution.py:217
  378.5 4.9 multiply_reduce_fusion.1
  383.5 2.0 fusion.100
  388.0 2.4 copy.95
  390.4 1.8 copy.114
  392.1 24.2 %all-gather.17.cloned.1.call-done = bf16[2048,768]{1,0:T(8,128)(2,1)} async-done(((bf16[512,768]{1,0:T(8,128)(2,1)}), bf16[2048,768]{1,0:T(8,128)(2,1)}) %all-gather.17.cloned.1.call-update) | async-done | bytes 3145744 | tf_op jit(solution)/shard_map/all_gather | solution.py:227
  416.4 3.5 fusion.70
  419.9 1.5 reshape.281
  422.7 32.6 %while.27 = (s32[]{:T(128)}, bf16[4,512,3,64]{1,3,2,0:T(8,128)(2,1)}, bf16[4,512,3,64]{1,3,2,0:T(8,128)(2,1)}, bf16[4,512,3,64]{1,3,2,0:T(8,128)(2,1)}, bf16[4,5...) while((s32[]{:T(128)}, ...), condition=%wide.region_17.18_spmd, body=%wide.region_15.17_spmd.sunk | while | flops 511408640 | bytes 26129024 | solution.py:232
  423.0 1.5 fusion.160
  431.2 1.5 fusion.160
  439.3 1.5 fusion.160
  447.5 1.5 fusion.160
  455.4 1.8 copy.98
  457.8 4.1 convolution_bitcast_fusion
  463.1 1.7 copy.99
  465.5 1.7 copy.100
  469.8 5.9 fusion.85
  475.6 4.3 copy.107
  479.9 4.8 reshape.286
  484.8 6.0 bitcast_convert_fusion
  490.9 7.0 fusion.106
  498.3 7.0 fusion.105
  505.5 39.8 %all-reduce.2 = (f32[1]{0:T(128)}, f32[1]{0:T(128)}, f32[1]{0:T(128)}, f32[1]{0:T(128)}) all-reduce(f32[1]{0:T(128)} %bitcast.37, f32[1]{0:T(128)} %bitcast.36, f32[1]{0:T(128)} %bitcast.35, f32[1]{0:T(128)} %bitcast.34), channel_id=1, replica_groups=mesh['dp'=8,'tensor'=4] {'dp','tensor'}, use_global_device_ids=true, to_apply=%region_43.44 | all-reduce | flops 4 | bytes 32 | tf_op jit(solution)/shard_map/pmax | solution.py:193
  545.4 3.2 fusion.96
  550.5 41.6 %all-reduce.1 = (f32[768]{0:T(1024)S(1)}, f32[768]{0:T(1024)S(1)}, f32[6,768]{1,0:T(8,128)S(1)}, f32[3072]{0:T(1024)S(1)}) all-reduce(f32[768]{0:T(1024)S(1)} %mul.303, f32[768]{0:T(1024)S(1)} %mul.298, f32[6,768]{1,0:T(8,128)S(1)} %stack.58, f32[3072]{0:T(1024)S(1)} %mul.309), channel_id=1, replica_groups=mesh['dp'=8,'tensor'=4] {'dp','tensor'}, use_global_device_ids=true, to_apply=%region_23.24 | all-reduce | flops 9216 | bytes 73728 | tf_op jit(solution)/shard_map/psum | solution.py:279
  594.2 1.6 copy.110
  597.7 36.6 %reduce-scatter.19.cloned.1.call-done = bf16[512,768]{1,0:T(8,128)(2,1)} async-done(((bf16[2048,768]{1,0:T(8,128)(2,1)}), bf16[512,768]{1,0:T(8,128)(2,1)}) %reduce-scatter.19.cloned.1.call-update) | async-done | bytes 786448 | tf_op jit(solution)/shard_map/reduce_scatter | solution.py:244
  634.3 2.9 add_convert_fusion
  637.2 70.8 %reduce-scatter.23.cloned.1.call-done = f32[768,96]{0,1:T(8,128)} async-done(((f32[768,768]{0,1:T(8,128)}), f32[768,96]{0,1:T(8,128)}) %reduce-scatter.23.cloned.1.call-update) | async-done | bytes 294928 | tf_op jit(solution)/shard_map/reduce_scatter | solution.py:259
  708.0 73.0 %reduce-scatter.21.cloned.1.call-done = f32[96,768]{1,0:T(8,128)} async-done(((f32[768,768]{1,0:T(8,128)}), f32[96,768]{1,0:T(8,128)}) %reduce-scatter.21.cloned.1.call-update) | async-done | bytes 294928 | tf_op jit(solution)/shard_map/reduce_scatter | solution.py:258
  (225 shorter events, 64.8 us)
Async XLA Ops:
  8.0 79.7 %all-gather.7.cloned.1.call-start = ((), (), s32[]{:S(2)}) async-start(), calls=%async_computation.8 | async-start | bytes 3932160 | tf_op jit(solution)/shard_map/all_gather | solution.py:163
  12.8 42.1 %copy-start.28 = (f32[2,192]{1,0:T(2,128)S(1)}, f32[2,192]{1,0:T(2,128)}, u32[]{:S(2)}) copy-start(f32[2,192]{1,0:T(2,128)} %param.24) | copy-start | bytes 4612
  12.8 42.9 %copy-start.29 = (s32[12]{0:T(128)S(1)}, s32[12]{0:T(128)}, u32[]{:S(2)}) copy-start(s32[12]{0:T(128)} %param.37) | copy-start | bytes 148
  12.8 43.7 %copy-start.14 = (f32[192,96]{1,0:T(8,128)S(1)}, f32[192,96]{1,0:T(8,128)}, u32[]{:S(2)}) copy-start(f32[192,96]{1,0:T(8,128)} %param.25) | copy-start | bytes 221188
  12.8 152.2 %reduce-scatter.13.cloned.1.call-start = ((), (), s32[]{:S(2)}) async-start(), calls=%async_computation.9 | async-start | bytes 3932160 | tf_op jit(solution)/shard_map/reduce_scatter | solution.py:172
  119.3 5.0 copy-start.6
  124.3 0.9 copy-start.8
  125.2 2.8 copy-start.12
  125.2 39.8 %copy-start = (bf16[512,768]{1,0:T(8,128)(2,1)S(1)}, bf16[512,768]{1,0:T(8,128)(2,1)}, u32[]{:S(2)}) copy-start(bf16[512,768]{1,0:T(8,128)(2,1)} %param.21) | copy-start | bytes 2359300
  125.2 39.8 %copy-start.13 = (f32[768]{0:T(1024)S(1)}, f32[768]{0:T(1024)}, u32[]{:S(2)}) copy-start(f32[768]{0:T(1024)} %param.26) | copy-start | bytes 9220
  127.9 45.5 %all-gather.11.cloned.1.call-start = ((), (), s32[]{:S(2)}) async-start(), calls=%async_computation.11 | async-start | bytes 1327104 | tf_op jit(solution)/shard_map/all_gather | solution.py:158
  128.7 71.7 %all-gather.9.cloned.1.call-start = ((), (), s32[]{:S(2)}) async-start(), calls=%async_computation.10 | async-start | bytes 3932160 | tf_op jit(solution)/shard_map/all_gather | solution.py:181
  165.0 3.7 copy-start.1
  166.5 1.6 copy-start.15
  168.1 0.6 copy-start.17
  171.6 72.9 %all-gather.13.cloned.1.call-start = ((), (), s32[]{:S(2)}) async-start(), calls=%async_computation.12 | async-start | bytes 1327104 | tf_op jit(solution)/shard_map/all_gather | solution.py:159
  173.3 113.9 %reduce-scatter.15.cloned.1.call-start = ((), (), s32[]{:S(2)}) async-start(), calls=%async_computation.13 | async-start | bytes 3932160 | tf_op jit(solution)/shard_map/reduce_scatter | solution.py:185
  218.3 2.7 copy-start.5
  251.0 72.9 %all-gather.15.cloned.1.call-start = ((), (), s32[]{:S(2)}) async-start(), calls=%async_computation.14 | async-start | bytes 3932160 | tf_op jit(solution)/shard_map/all_gather | solution.py:206
  287.2 2.3 copy-start.10
  287.2 2.3 copy-start.20
  287.2 3.7 copy-start.27
  293.0 1.2 copy-start.4
  295.2 83.3 %reduce-scatter.17.cloned.1.call-start = ((), (), s32[]{:S(2)}) async-start(), calls=%async_computation.15 | async-start | bytes 3932160 | tf_op jit(solution)/shard_map/reduce_scatter | solution.py:217
  323.9 12.7 %copy-start.30 = (bf16[768,768]{1,0:T(8,128)(2,1)S(1)}, bf16[768,768]{1,0:T(8,128)(2,1)}, u32[]{:S(2)}) copy-start(bf16[768,768]{1,0:T(8,128)(2,1)} %all-gather.11.cloned.1.call-done) | copy-start | bytes 3538948
  335.0 1.7 copy-start.31
  340.7 75.6 %all-gather.17.cloned.1.call-start = ((), (), s32[]{:S(2)}) async-start(), calls=%async_computation.16 | async-start | bytes 3932160 | tf_op jit(solution)/shard_map/all_gather | solution.py:227
  378.5 4.9 copy-start.16
  385.4 1.2 copy-start.2
  387.7 206.5 %reduce-scatter.27.cloned.1.call-start = ((), (), s32[]{:S(2)}) async-start(), calls=%async_computation.21 | async-start | bytes 884736
  455.4 2.4 copy-start.9
  461.9 133.9 %reduce-scatter.25.cloned.1.call-start = ((), (), s32[]{:S(2)}) async-start(), calls=%async_computation.20 | async-start | bytes 2211840
  479.9 4.9 copy-start.11
  484.7 149.6 %reduce-scatter.19.cloned.1.call-start = ((), (), s32[]{:S(2)}) async-start(), calls=%async_computation.17 | async-start | bytes 3932160 | tf_op jit(solution)/shard_map/reduce_scatter | solution.py:244
  490.8 217.2 %reduce-scatter.23.cloned.1.call-start = ((), (), s32[]{:S(2)}) async-start(), calls=%async_computation.19 | async-start | bytes 2654208 | tf_op jit(solution)/shard_map/reduce_scatter | solution.py:259
  497.9 7.5 copy-start.21
  497.9 7.5 copy-start.19
  497.9 7.5 copy-start.18
  497.9 7.5 copy-start.26
  497.9 47.4 %copy-start.24 = (f32[768]{0:T(1024)S(1)}, f32[768]{0:T(1024)}, u32[]{:S(2)}) copy-start(f32[768]{0:T(1024)} %get-tuple-element.326) | copy-start | bytes 9220
  497.9 47.4 %copy-start.23 = (f32[768]{0:T(1024)S(1)}, f32[768]{0:T(1024)}, u32[]{:S(2)}) copy-start(f32[768]{0:T(1024)} %get-tuple-element.258) | copy-start | bytes 9220
  497.9 47.4 %copy-start.22 = (f32[768]{0:T(1024)S(1)}, f32[768]{0:T(1024)}, u32[]{:S(2)}) copy-start(f32[768]{0:T(1024)} %get-tuple-element.264) | copy-start | bytes 9220
  498.0 47.4 %copy-start.25 = (f32[4]{0:T(128)S(1)}, f32[4]{0:T(128)}, u32[]{:S(2)}) copy-start(f32[4]{0:T(128)} %param.35) | copy-start | bytes 52
  498.0 50.6 %copy-start.7 = (bf16[4,512,3,64]{1,3,2,0:T(8,128)(2,1)S(1)}, bf16[4,512,3,64]{1,3,2,0:T(8,128)(2,1)}, u32[]{:S(2)}) copy-start(bf16[4,512,3,64]{1,3,2,0:T(8,128)(2,1)} %get-tuple-element.119) | copy-start | bytes 2359300
  498.0 283.1 %reduce-scatter.21.cloned.1.call-start = ((), (), s32[]{:S(2)}) async-start(), calls=%async_computation.18 | async-start | bytes 2654208 | tf_op jit(solution)/shard_map/reduce_scatter | solution.py:258
  505.3 129.0 %copy-start.3 = (f32[512,768]{1,0:T(8,128)S(1)}, f32[512,768]{1,0:T(8,128)}, u32[]{:S(2)}) copy-start(f32[512,768]{1,0:T(8,128)} %copy-done.2) | copy-start | bytes 4718596
Sparse Core Ops, SparseCore 0:
  12.9 31.2 all-gather.6
  128.0 36.8 reduce-scatter.12
  295.4 28.5 all-gather.14
  387.8 28.4 all-gather.16
Sparse Core Ops, SparseCore 1:
  131.2 40.4 all-gather.10
  173.6 26.7 all-gather.8
  203.0 41.4 all-gather.12
  251.1 36.1 reduce-scatter.14
  340.8 37.7 reduce-scatter.16
  462.0 63.3 reduce-scatter.26
  528.7 66.4 reduce-scatter.24
  597.6 36.7 reduce-scatter.18
  638.3 69.7 reduce-scatter.22
  712.1 68.9 reduce-scatter.20
where the time goes:
time: 799 us; the launch traced here: 789 us
  waiting for transfers between devices  390 us (49%)
  blocking collectives  151 us (19%)
  matrix products  116 us (15%)
  other arithmetic  56.4 us (7%)
  local copies, waits for them, and re-layouts  55.7 us (7%)
  between operations  17.5 us (2%)
    reduce_scatter x1, waiting for transfers between devices, body(): lax.psum_scatter(up_grad, 'dp', scatter_dimension=0, tiled=True)  73 us
    reduce_scatter x1, waiting for transfers between devices, body(): lax.psum_scatter(down_grad, 'dp', scatter_dimension=1, tiled=True)  70.8 us
    psum x1, blocking collectives, body(): lax.psum((spread(query_bias_part), spread(value_bias_part), spread(up_bia...  41.6 us
    pmax x1, blocking collectives, body(): lax.pmax((jnp.max(jnp.abs(inputs)), jnp.max(jnp.abs(context)), jnp.max(jn...  39.8 us
    all_gather x1, blocking collectives, body(): lax.all_gather(masters[0], 'dp', axis=1, tiled=True)  38.9 us
    reduce_scatter x1, waiting for transfers between devices, body(): lax.psum_scatter(matmul_right_t(grad_up, up_back).astype(jnp.bfloat16), '...  37.8 us
    reduce_scatter x1, waiting for transfers between devices, body(): lax.psum_scatter(jnp.einsum('jte,jde->td', stacked, qkv_back, preferred_e...  36.6 us
    reduce_scatter x1, waiting for transfers between devices, body(): lax.psum_scatter(matmul_plain(ctx_clip, out_full).astype(jnp.bfloat16), '...  36 us
  transfers between devices with their start and end apart: 14, of which 10 were waited for; matrix products, arithmetic and copies ran while one was open for 12% of the time, Pallas kernels for 0%

commit v1 on v0

--- a/solution.py
+++ b/solution.py
@@ -10,6 +10,27 @@
 epsilon = 1e-06
 root_half = 0.7071067811865476
 density_scale = 0.3989422804014327
+
+
+def review_members_all_by_axis(frame_in):
+    comm_axis = "dp"
+    parts_seen = []
+    workers = jax.lax.axis_size(comm_axis)
+    for it in range(workers):
+        parts_seen.append((it, (it + 1) % workers))
+    sides = []
+    for it in range(workers):
+        sides.append((it, (it - 1) % workers))
+    res, a_now = ([frame_in], [frame_in])
+    for _ in range(workers // 2):
+        x_next = jax.lax.ppermute(res[-1], axis_name=comm_axis, perm=parts_seen)
+        res.append(x_next)
+    for _ in range((workers - 1) // 2):
+        a_now.append(jax.lax.ppermute(a_now[-1], axis_name=comm_axis, perm=sides))
+    carry_out = jnp.concatenate([*res[::-1], *a_now[1:]], 1)
+    everything = jax.lax.axis_index(comm_axis)
+    prior = jnp.roll(carry_out, (everything - workers // 2) * frame_in.shape[1], 1)
+    return prior
 
 
 def matmul_plain(left, right):
@@ -154,7 +175,7 @@
     )
     qkv_full, out_full, up_full, down_full = (
         lax.all_gather(masters[0], "dp", axis=1, tiled=True),
-        lax.all_gather(masters[1], "dp", axis=1, tiled=True),
+        review_members_all_by_axis(masters[1]),
         lax.all_gather(masters[2], "dp", axis=0, tiled=True),
         lax.all_gather(masters[3], "dp", axis=1, tiled=True),
     )

time: 799 us -> 807 us (1.010)
  starting transfers between devices: 1.86 us -> 17.4 us
  waiting for transfers between devices: 390 us -> 380 us
    all_gather x1, waiting for transfers between devices: 24.2 us -> 0.01 us  [body(): lax.all_gather(grad_first.astype(jnp.bfloat16), 'tensor', axis=0, tiled=T...]
    ppermute x0 -> x7, starting transfers between devices: none -> 15.8 us  [the longest x3 12.6 us: review_members_all_by_axis(): a_now.append(jax.lax.ppermute(a_now[-1], axis_name=comm_axis, perm=sides))]
    ppermute x0 -> x7, waiting for transfers between devices: none -> 9.31 us  [the longest x4 9.31 us: review_members_all_by_axis(): x_next = jax.lax.ppermute(res[-1], axis_name=comm_axis, perm=parts_seen)]
    unnamed x75 -> x98, local copies, waits for them, and re-layouts: 24.9 us -> 33.9 us
  transfers between devices with their start and end apart: 14 -> 21, of which waited for: 10 -> 14; matrix products, arithmetic and copies ran while one was open for 12% -> 12% of each run, Pallas kernels for 0% -> 0%
where the time goes in v1:
time: 807 us; the launch traced here: 796 us
  waiting for transfers between devices  380 us (47%)
  blocking collectives  149 us (18%)
  matrix products  115 us (14%)
  local copies, waits for them, and re-layouts  62.5 us (8%)
  other arithmetic  53.8 us (7%)
  between operations  17.7 us (2%)
  starting transfers between devices  17.4 us (2%)
    reduce_scatter x1, waiting for transfers between devices, body(): lax.psum_scatter(up_grad, 'dp', scatter_dimension=0, tiled=True)  73 us
    reduce_scatter x1, waiting for transfers between devices, body(): lax.psum_scatter(down_grad, 'dp', scatter_dimension=1, tiled=True)  70.9 us
    psum x1, blocking collectives, body(): lax.psum((spread(query_bias_part), spread(value_bias_part), spread(up_bia...  42.1 us
    pmax x1, blocking collectives, body(): lax.pmax((jnp.max(jnp.abs(inputs)), jnp.max(jnp.abs(context)), jnp.max(jn...  39.3 us
    reduce_scatter x1, waiting for transfers between devices, body(): lax.psum_scatter(matmul_right_t(grad_up, up_back).astype(jnp.bfloat16), '...  37.8 us
    reduce_scatter x1, waiting for transfers between devices, body(): lax.psum_scatter(jnp.einsum('jte,jde->td', stacked, qkv_back, preferred_e...  37 us
    all_gather x1, blocking collectives, body(): lax.all_gather(masters[0], 'dp', axis=1, tiled=True)  36.5 us
    reduce_scatter x1, waiting for transfers between devices, body(): lax.psum_scatter(matmul_plain(act_clip, down_full).astype(jnp.bfloat16),...  35.7 us
  transfers between devices with their start and end apart: 21, of which 14 were waited for; matrix products, arithmetic and copies ran while one was open for 12% of the time, Pallas kernels for 0%

profile of v1, /device:TPU:0, one launch (start us, length us, event | category | flops | bytes accessed | tf_op | source)
XLA Modules:
  0.0 796.1 jit_solution(3589021952459809245)
XLA Ops:
  10.0 2.8 fusion.80
  13.9 3.0 collective-permute-start
  16.9 3.1 collective-permute-start.4
  21.3 36.5 %all_gather.28 = bf16[3,768,192]{2,0,1:T(4,128)(2,1)S(1)} all-gather(bf16[3,96,192]{2,0,1:T(4,128)(2,1)S(1)} %copy.88), channel_id=1, replica_groups=mesh['dp'=8,'tensor'=4] {'dp'}, dimensions={1}, use_global_device_ids=true | all-gather | bytes 995328 | tf_op jit(solution)/shard_map/all_gather | solution.py:177
  58.6 6.4 collective-permute-done.1
  65.0 4.8 collective-permute-start.5
  69.8 2.0 collective-permute-done.2
  72.9 4.8 collective-permute-start.6
  88.6 3.9 fusion.106
  94.0 3.2 squeeze.75
  97.1 2.2 squeeze.76
  100.1 2.9 fusion.83
  103.0 16.9 %while.26 = (s32[]{:T(128)}, f32[4,512,3,64]{1,3,2,0:T(8,128)}, f32[4,3,512]{2,1,0:T(4,128)}, bf16[4,512,3,64]{1,3,2,0:T(8,128)(2,1)S(1)}, s32[4,512]{1,0:T(4,12...) while((s32[]{:T(128)}, f32[4,512,3,64]{1,3,2,0:T(8,128)}, ...), condition=%wide.region_3.4_spmd, body=%wide.region_0.3_spmd.sunk | while | flops 211286528 | bytes 11534437 | solution.py:190
  105.4 1.8 fusion.152
  109.6 1.8 fusion.152
  113.8 1.8 fusion.152
  118.1 1.8 fusion.152
  119.9 4.2 abs_reduce_fusion.2
  125.7 3.7 convolution_convert_fusion.2
  131.4 34.8 %reduce-scatter.13.cloned.1.call-done = bf16[512,768]{1,0:T(8,128)(2,1)} async-done(((bf16[2048,768]{1,0:T(8,128)(2,1)}), bf16[512,768]{1,0:T(8,128)(2,1)}) %reduce-scatter.13.cloned.1.call-update) | async-done | bytes 786448 | tf_op jit(solution)/shard_map/reduce_scatter | solution.py:193
  167.8 1.6 multiply_reduce_fusion.4
  169.4 2.2 multiply_convert_fusion.2
  172.8 28.8 %all-gather.9.cloned.1.call-done = bf16[2048,768]{1,0:T(8,128)(2,1)} async-done(((bf16[512,768]{1,0:T(8,128)(2,1)}), bf16[2048,768]{1,0:T(8,128)(2,1)}) %all-gather.9.cloned.1.call-update) | async-done | bytes 3145744 | tf_op jit(solution)/shard_map/all_gather | solution.py:202
  201.6 17.8 %abs_reduce_fusion = (f32[]{:T(128)}, f32[2048,768]{1,0:T(8,128)S(1)}, f32[2048,768]{1,0:T(8,128)}) fusion(f32[768]{0:T(1024)S(1)} %copy-done.34, bf16[2048,768]{1,0:T(8,128)(2,1)} %all-gather.9.cloned.1.call-done, bf16[768,768]{1,0:T(8,128)(2,1)} %all-gather.11.cloned.1.call-done), kind=kOutput, calls=%fused_computation.74 | convolution fusion | flops 2521300992 | bytes 16911364 | tf_op jit(solution)/shard_map/dot_general | solution.py:37
  219.4 2.7 copy-done.7
  222.1 3.6 multiply_convert_fusion.1
  225.7 20.0 %all-gather.13.cloned.1.call-done = bf16[768,768]{0,1:T(8,128)(2,1)} async-done(((bf16[768,96]{0,1:T(8,128)(2,1)}), bf16[768,768]{0,1:T(8,128)(2,1)}) %all-gather.13.cloned.1.call-update) | async-done | bytes 1179664 | tf_op jit(solution)/shard_map/all_gather | solution.py:180
  245.7 6.5 convolution_convert_fusion.1
  252.7 35.7 %reduce-scatter.15.cloned.1.call-done = bf16[512,768]{1,0:T(8,128)(2,1)} async-done(((bf16[2048,768]{1,0:T(8,128)(2,1)}), bf16[512,768]{1,0:T(8,128)(2,1)}) %reduce-scatter.15.cloned.1.call-update) | async-done | bytes 786448 | tf_op jit(solution)/shard_map/reduce_scatter | solution.py:206
  288.4 2.0 fusion.103
  292.1 2.1 fusion.100
  296.5 28.6 %all-gather.15.cloned.1.call-done = bf16[2048,768]{1,0:T(8,128)(2,1)} async-done(((bf16[512,768]{1,0:T(8,128)(2,1)}), bf16[2048,768]{1,0:T(8,128)(2,1)}) %all-gather.15.cloned.1.call-update) | async-done | bytes 3145744 | tf_op jit(solution)/shard_map/all_gather | solution.py:227
  325.1 11.1 %convert_reduce_fusion = (f32[768]{0:T(1024)}, bf16[2048,768]{1,0:T(8,128)(2,1)S(1)}) fusion(f32[2048,768]{1,0:T(8,128)} %get-tuple-element.347, f32[768]{0:T(1024)S(1)} %copy-done.34, f32[2048,768]{1,0:T(8,128)} %copy-done.7, f32[]{:T(128)} %bitcast.27, bf16[2048,768]{1,0:T(8,128)(2,1)} %all-gather.15.cloned.1.call-done, ...), kind=kOutput, calls=%fused_computation.75 | convolution fusion | flops 2442657024 | bytes 20060164 | tf_op jit(solution)/shard_map/dot_general | solution.py:47
  336.2 1.7 copy-done.35
  337.8 4.0 convolution_convert_fusion
  341.9 37.8 %reduce-scatter.17.cloned.1.call-done = bf16[512,768]{1,0:T(8,128)(2,1)} async-done(((bf16[2048,768]{1,0:T(8,128)(2,1)}), bf16[512,768]{1,0:T(8,128)(2,1)}) %reduce-scatter.17.cloned.1.call-update) | async-done | bytes 786448 | tf_op jit(solution)/shard_map/reduce_scatter | solution.py:238
  379.7 4.8 multiply_reduce_fusion.1
  388.2 31.5 %all_gather.34 = bf16[192,768]{0,1:T(8,128)(2,1)S(1)} all-gather(bf16[192,96]{0,1:T(8,128)(2,1)S(1)} %copy-done.15), channel_id=1, replica_groups=mesh['dp'=8,'tensor'=4] {'dp'}, dimensions={1}, use_global_device_ids=true | all-gather | bytes 331776 | tf_op jit(solution)/shard_map/all_gather | solution.py:230
  419.7 2.4 copy.95
  422.1 1.8 copy.114
  423.8 3.5 fusion.70
  430.2 32.6 %while.27 = (s32[]{:T(128)}, bf16[4,512,3,64]{1,3,2,0:T(8,128)(2,1)}, bf16[4,512,3,64]{1,3,2,0:T(8,128)(2,1)}, bf16[4,512,3,64]{1,3,2,0:T(8,128)(2,1)}, bf16[4,5...) while((s32[]{:T(128)}, ...), condition=%wide.region_17.18_spmd, body=%wide.region_15.17_spmd.sunk | while | flops 511408640 | bytes 26129024 | solution.py:253
  430.5 1.5 fusion.161
  438.6 1.5 fusion.161
  446.8 1.5 fusion.161
  454.9 1.5 fusion.161
  462.8 1.8 copy.98
  465.2 4.2 convolution_bitcast_fusion
  471.9 1.7 copy.100
  476.1 4.6 fusion.85
  480.7 2.8 copy.107
  483.5 4.8 reshape.286
  488.4 6.1 bitcast_convert_fusion
  494.5 7.0 fusion.108
  501.9 7.0 fusion.107
  509.1 39.3 %all-reduce.2 = (f32[1]{0:T(128)}, f32[1]{0:T(128)}, f32[1]{0:T(128)}, f32[1]{0:T(128)}) all-reduce(f32[1]{0:T(128)} %bitcast.37, f32[1]{0:T(128)} %bitcast.36, f32[1]{0:T(128)} %bitcast.35, f32[1]{0:T(128)} %bitcast.34), channel_id=1, replica_groups=mesh['dp'=8,'tensor'=4] {'dp','tensor'}, use_global_device_ids=true, to_apply=%region_43.44 | all-reduce | flops 4 | bytes 32 | tf_op jit(solution)/shard_map/pmax | solution.py:214
  548.5 3.2 fusion.97
  553.6 42.1 %all-reduce.1 = (f32[768]{0:T(1024)S(1)}, f32[768]{0:T(1024)S(1)}, f32[6,768]{1,0:T(8,128)S(1)}, f32[3072]{0:T(1024)S(1)}) all-reduce(f32[768]{0:T(1024)S(1)} %mul.307, f32[768]{0:T(1024)S(1)} %mul.302, f32[6,768]{1,0:T(8,128)S(1)} %stack.58, f32[3072]{0:T(1024)S(1)} %mul.313), channel_id=1, replica_groups=mesh['dp'=8,'tensor'=4] {'dp','tensor'}, use_global_device_ids=true, to_apply=%region_23.24 | all-reduce | flops 9216 | bytes 73728 | tf_op jit(solution)/shard_map/psum | solution.py:300
  597.8 1.6 copy.110
  599.4 3.5 reduce-scatter.25.cloned.1.call-done
  604.8 37.0 %reduce-scatter.19.cloned.1.call-done = bf16[512,768]{1,0:T(8,128)(2,1)} async-done(((bf16[2048,768]{1,0:T(8,128)(2,1)}), bf16[512,768]{1,0:T(8,128)(2,1)}) %reduce-scatter.19.cloned.1.call-update) | async-done | bytes 786448 | tf_op jit(solution)/shard_map/reduce_scatter | solution.py:265
  641.8 2.9 add_convert_fusion
  644.7 70.9 %reduce-scatter.23.cloned.1.call-done = f32[768,96]{0,1:T(8,128)} async-done(((f32[768,768]{0,1:T(8,128)}), f32[768,96]{0,1:T(8,128)}) %reduce-scatter.23.cloned.1.call-update) | async-done | bytes 294928 | tf_op jit(solution)/shard_map/reduce_scatter | solution.py:280
  715.5 73.0 %reduce-scatter.21.cloned.1.call-done = f32[96,768]{1,0:T(8,128)} async-done(((f32[768,768]{1,0:T(8,128)}), f32[96,768]{1,0:T(8,128)}) %reduce-scatter.21.cloned.1.call-update) | async-done | bytes 294928 | tf_op jit(solution)/shard_map/reduce_scatter | solution.py:279
  (263 shorter events, 82.9 us)
Async XLA Ops:
  8.0 13.1 %copy-start.32 = (s32[12]{0:T(128)S(1)}, s32[12]{0:T(128)}, u32[]{:S(2)}) copy-start(s32[12]{0:T(128)} %param.37) | copy-start | bytes 148
  8.0 49.8 %copy-start.31 = (f32[2,192]{1,0:T(2,128)S(1)}, f32[2,192]{1,0:T(2,128)}, u32[]{:S(2)}) copy-start(f32[2,192]{1,0:T(2,128)} %param.24) | copy-start | bytes 4612
  8.0 80.5 %all-gather.7.cloned.1.call-start = ((), (), s32[]{:S(2)}) async-start(), calls=%async_computation.8 | async-start | bytes 3932160 | tf_op jit(solution)/shard_map/all_gather | solution.py:184
  12.8 153.4 %reduce-scatter.13.cloned.1.call-start = ((), (), s32[]{:S(2)}) async-start(), calls=%async_computation.9 | async-start | bytes 3932160 | tf_op jit(solution)/shard_map/reduce_scatter | solution.py:193
  13.9 72.2 %copy-start.14 = (bf16[192,96]{0,1:T(8,128)(2,1)}, bf16[192,96]{0,1:T(8,128)(2,1)S(1)}, u32[]{:S(2)}) copy-start(bf16[192,96]{0,1:T(8,128)(2,1)S(1)} %copy.94) | copy-start | bytes 110596
  13.9 44.0 %collective-permute-start = (bf16[192,96]{0,1:T(8,128)(2,1)S(1)}, bf16[192,96]{0,1:T(8,128)(2,1)S(1)}, u32[]{:S(2)}, u32[]{:S(2)}) collective-permute-start(bf16[192,96]{0,1:T(8,128)(2,1)S(1)} %copy.94), channel_id=1, source_target_pairs={{0,4},{4,8},{8,12},{12,16},{16,20},{20,24},{24,28},{28,0},{1,5},{5... | collective-permute-start | bytes 110600 | tf_op jit(solution)/shard_map/ppermute | solution.py:26
  16.9 48.1 %collective-permute-start.4 = (bf16[192,96]{0,1:T(8,128)(2,1)S(1)}, bf16[192,96]{0,1:T(8,128)(2,1)S(1)}, u32[]{:S(2)}, u32[]{:S(2)}) collective-permute-start(bf16[192,96]{0,1:T(8,128)(2,1)S(1)} %copy.94), channel_id=1, source_target_pairs={{0,28},{4,0},{8,4},{12,8},{16,12},{20,16},{24,20},{28,24},{1,29},{... | collective-permute-start | bytes 110600 | tf_op jit(solution)/shard_map/ppermute | solution.py:29
  57.8 7.2 collective-permute-start.1
  65.0 6.8 collective-permute-start.2
  65.0 7.9 collective-permute-start.5
  71.8 6.8 collective-permute-start.3
  72.7 19.8 %copy-start.11 = (bf16[3,768,192]{1,2,0:T(8,128)(2,1)}, bf16[3,768,192]{1,2,0:T(8,128)(2,1)S(1)}, u32[]{:S(2)}) copy-start(bf16[3,768,192]{1,2,0:T(8,128)(2,1)S(1)} %copy.89) | copy-start | bytes 2654212
  72.9 10.0 %collective-permute-start.6 = (bf16[192,96]{0,1:T(8,128)(2,1)S(1)}, bf16[192,96]{0,1:T(8,128)(2,1)S(1)}, u32[]{:S(2)}, u32[]{:S(2)}) collective-permute-start(bf16[192,96]{0,1:T(8,128)(2,1)S(1)} %collective-permute-done.5), channel_id=1, source_target_pairs={{0,28},{4,0},{8,4},{12,8},{16,12},{20,16},{24,20},{28,24},{1,29},{... | collective-permute-start | bytes 110600 | tf_op jit(solution)/shard_map/ppermute | solution.py:29
  119.9 5.0 copy-start.8
  124.9 0.9 copy-start.5
  129.5 1.0 copy-start.16
  129.5 36.8 %copy-start = (bf16[512,768]{1,0:T(8,128)(2,1)S(1)}, bf16[512,768]{1,0:T(8,128)(2,1)}, u32[]{:S(2)}) copy-start(bf16[512,768]{1,0:T(8,128)(2,1)} %param.21) | copy-start | bytes 2359300
  129.5 36.8 %copy-start.18 = (f32[768]{0:T(1024)S(1)}, f32[768]{0:T(1024)}, u32[]{:S(2)}) copy-start(f32[768]{0:T(1024)} %param.26) | copy-start | bytes 9220
  129.5 39.9 %copy-start.19 = (f32[768]{0:T(1024)S(1)}, f32[768]{0:T(1024)}, u32[]{:S(2)}) copy-start(f32[768]{0:T(1024)} %param.27) | copy-start | bytes 9220
  129.5 39.9 %copy-start.20 = (f32[768]{0:T(1024)S(1)}, f32[768]{0:T(1024)}, u32[]{:S(2)}) copy-start(f32[768]{0:T(1024)} %param.28) | copy-start | bytes 9220
  129.5 43.3 %all-gather.11.cloned.1.call-start = ((), (), s32[]{:S(2)}) async-start(), calls=%async_computation.11 | async-start | bytes 1327104 | tf_op jit(solution)/shard_map/all_gather | solution.py:179
  131.1 40.5 %copy-start.17 = (f32[768,96]{0,1:T(8,128)S(1)}, f32[768,96]{0,1:T(8,128)}, u32[]{:S(2)}) copy-start(f32[768,96]{0,1:T(8,128)} %param.31) | copy-start | bytes 884740
  131.1 70.4 %copy-start.34 = (f32[768]{0:T(1024)S(1)}, f32[768]{0:T(1024)}, u32[]{:S(2)}) copy-start(f32[768]{0:T(1024)} %param.30) | copy-start | bytes 9220
  131.2 70.4 %all-gather.9.cloned.1.call-start = ((), (), s32[]{:S(2)}) async-start(), calls=%async_computation.10 | async-start | bytes 3932160 | tf_op jit(solution)/shard_map/all_gather | solution.py:202
  166.3 3.2 copy-start.1
  171.6 74.0 %all-gather.13.cloned.1.call-start = ((), (), s32[]{:S(2)}) async-start(), calls=%async_computation.12 | async-start | bytes 1327104 | tf_op jit(solution)/shard_map/all_gather | solution.py:180
  172.4 116.0 %reduce-scatter.15.cloned.1.call-start = ((), (), s32[]{:S(2)}) async-start(), calls=%async_computation.13 | async-start | bytes 3932160 | tf_op jit(solution)/shard_map/reduce_scatter | solution.py:206
  219.4 2.7 copy-start.7
  252.2 36.2 %copy-start.29 = (f32[768]{0:T(1024)S(1)}, f32[768]{0:T(1024)}, u32[]{:S(2)}) copy-start(f32[768]{0:T(1024)} %param.32) | copy-start | bytes 9220
  252.2 38.5 %copy-start.22 = (f32[768]{0:T(1024)S(1)}, f32[768]{0:T(1024)}, u32[]{:S(2)}) copy-start(f32[768]{0:T(1024)} %param.33) | copy-start | bytes 9220
  252.2 39.8 %copy-start.30 = (f32[768]{0:T(1024)S(1)}, f32[768]{0:T(1024)}, u32[]{:S(2)}) copy-start(f32[768]{0:T(1024)} %param.34) | copy-start | bytes 9220
  252.2 72.8 %all-gather.15.cloned.1.call-start = ((), (), s32[]{:S(2)}) async-start(), calls=%async_computation.14 | async-start | bytes 3932160 | tf_op jit(solution)/shard_map/all_gather | solution.py:227
  288.4 2.3 copy-start.10
  294.2 1.2 copy-start.4
  296.4 83.3 %reduce-scatter.17.cloned.1.call-start = ((), (), s32[]{:S(2)}) async-start(), calls=%async_computation.15 | async-start | bytes 3932160 | tf_op jit(solution)/shard_map/reduce_scatter | solution.py:238
  325.1 12.7 %copy-start.33 = (bf16[768,768]{1,0:T(8,128)(2,1)S(1)}, bf16[768,768]{1,0:T(8,128)(2,1)}, u32[]{:S(2)}) copy-start(bf16[768,768]{1,0:T(8,128)(2,1)} %all-gather.11.cloned.1.call-done) | copy-start | bytes 3538948
  336.1 1.7 copy-start.35
  341.9 82.0 %all-gather.17.cloned.1.call-start = ((), (), s32[]{:S(2)}) async-start(), calls=%async_computation.16 | async-start | bytes 3932160 | tf_op jit(solution)/shard_map/all_gather | solution.py:248
  385.8 1.2 copy-start.2
  385.8 2.4 copy-start.15
  388.1 209.6 %reduce-scatter.27.cloned.1.call-start = ((), (), s32[]{:S(2)}) async-start(), calls=%async_computation.21 | async-start | bytes 884736
  462.8 2.4 copy-start.6
  465.2 5.4 copy-start.13
  469.5 133.4 %reduce-scatter.25.cloned.1.call-start = ((), (), s32[]{:S(2)}) async-start(), calls=%async_computation.20 | async-start | bytes 2211840
  483.5 4.9 copy-start.12
  488.3 153.5 %reduce-scatter.19.cloned.1.call-start = ((), (), s32[]{:S(2)}) async-start(), calls=%async_computation.17 | async-start | bytes 3932160 | tf_op jit(solution)/shard_map/reduce_scatter | solution.py:265
  494.5 221.1 %reduce-scatter.23.cloned.1.call-start = ((), (), s32[]{:S(2)}) async-start(), calls=%async_computation.19 | async-start | bytes 2654208 | tf_op jit(solution)/shard_map/reduce_scatter | solution.py:280
  501.5 7.4 copy-start.23
  501.5 7.5 copy-start.21
  501.5 7.5 copy-start.28
  501.5 46.9 %copy-start.26 = (f32[768]{0:T(1024)S(1)}, f32[768]{0:T(1024)}, u32[]{:S(2)}) copy-start(f32[768]{0:T(1024)} %get-tuple-element.326) | copy-start | bytes 9220
  501.5 46.9 %copy-start.25 = (f32[768]{0:T(1024)S(1)}, f32[768]{0:T(1024)}, u32[]{:S(2)}) copy-start(f32[768]{0:T(1024)} %get-tuple-element.258) | copy-start | bytes 9220
  501.6 46.9 %copy-start.24 = (f32[768]{0:T(1024)S(1)}, f32[768]{0:T(1024)}, u32[]{:S(2)}) copy-start(f32[768]{0:T(1024)} %get-tuple-element.264) | copy-start | bytes 9220
  501.6 47.0 %copy-start.27 = (f32[4]{0:T(128)S(1)}, f32[4]{0:T(128)}, u32[]{:S(2)}) copy-start(f32[4]{0:T(128)} %param.35) | copy-start | bytes 52
  501.6 50.1 %copy-start.9 = (bf16[4,512,3,64]{1,3,2,0:T(8,128)(2,1)S(1)}, bf16[4,512,3,64]{1,3,2,0:T(8,128)(2,1)}, u32[]{:S(2)}) copy-start(bf16[4,512,3,64]{1,3,2,0:T(8,128)(2,1)} %get-tuple-element.119) | copy-start | bytes 2359300
  501.6 287.0 %reduce-scatter.21.cloned.1.call-start = ((), (), s32[]{:S(2)}) async-start(), calls=%async_computation.18 | async-start | bytes 2654208 | tf_op jit(solution)/shard_map/reduce_scatter | solution.py:279
  508.9 132.9 %copy-start.3 = (f32[512,768]{1,0:T(8,128)S(1)}, f32[512,768]{1,0:T(8,128)}, u32[]{:S(2)}) copy-start(f32[512,768]{1,0:T(8,128)} %copy-done.2) | copy-start | bytes 4718596
Sparse Core Ops, SparseCore 0:
  12.9 31.2 all-gather.6
  129.6 36.5 reduce-scatter.12
  296.5 28.5 all-gather.14
  388.2 28.4 all-gather.16
Sparse Core Ops, SparseCore 1:
  132.8 40.0 all-gather.10
  174.8 26.7 all-gather.8
  204.2 41.4 all-gather.12
  252.3 36.0 reduce-scatter.14
  342.0 37.7 reduce-scatter.16
  469.5 63.2 reduce-scatter.26
  536.2 66.6 reduce-scatter.24
  605.3 36.4 reduce-scatter.18
  645.7 69.8 reduce-scatter.22
  719.6 68.9 reduce-scatter.20
